TPU v7x, 512 devices: a whole 4x8x8 slice. The times are simulated.
512 devices in a mesh: rows: 64 (over x, y, core), cols: 8 (over z).
Axes of the slice: x: 4, y: 8, z: 8, core: 2. Of those that a mesh axis runs over, the one named last changes fastest.
Arguments:
- eigvecs: float32 [65536, 2048], P(('rows', 'cols')), may hold values from -6 to 6
- panels: float32 [8, 65536, 256], P('cols', 'rows'), may hold values from -0.375 to 0.375
- tfactors: float32 [2, 256, 256], replicated, may hold values from -0.03125 to 0.03125
- owners: int32 [2], replicated, may hold values from 0 to 7, as said below
Outputs:
- backvecs: float32 [65536, 2048], P('rows', 'cols')
Inputs may be any that keep to these rules, and one draw needn't show every extreme that they name: `owners`: the entries are distinct slots, among them 0 and 7.
All inputs are finite; a program needn't handle non-finite values.
Results may differ from a plain program's by a relative error of at most 0.00011.
Values sent between devices are 32-bit elements; how exact they have to be, the bound alone decides.
No kernel may reach another device: no remote copies, remote signals or barrier semaphores. Data moves between devices by JAX's collectives and lax.ppermute only.
A program may use at most 64 MiB of HBM per device.

v0:
```python
import jax
import jax.numpy as jnp
from jax import lax
from jax.sharding import PartitionSpec as P


def broadcast(x, axis, root):
    mine = lax.axis_index(axis) == root
    return lax.psum(jnp.where(mine, x, jnp.zeros_like(x)), axis)


def matmul(left, right):
    return jnp.dot(left, right, precision=lax.Precision.HIGHEST, preferred_element_type=jnp.float32)


def per_device(eigvecs, panels, tfactors, owners):
    tiles = lax.all_to_all(eigvecs, "cols", split_axis=1, concat_axis=0, tiled=True)
    count = tfactors.shape[0]
    local = panels[0]
    vectors = []
    for index in range(count):
        vectors.append(broadcast(local, "cols", owners[index]))
    factors = [jnp.triu(tfactors[index]) for index in range(count)]
    result = tiles
    for index in range(count):
        proj = lax.psum(matmul(vectors[index].T, result), "rows")
        coeff = matmul(factors[index], proj)
        result = result - matmul(vectors[index], coeff)
    return result


def solution(mesh):
    placed = (P(("rows", "cols"), None), P("cols", "rows", None), P(), P())
    return jax.shard_map(
        per_device, mesh=mesh, in_specs=placed, out_specs=P("rows", "cols"), check_vma=False
    )
```

profile of v0, /device:TPU:1, one launch (start us, length us, event | category | flops | bytes accessed | tf_op | source)
XLA Modules:
  0.0 508.5 jit_solution(2413982245606252921)
XLA Ops:
  6.5 0.0 all-reduce.9.cloned.1.call-start
  6.5 0.0 copy-start.4
  6.5 0.7 copy-done.4
  7.2 0.6 fusion.10
  9.1 2.7 select_bitcast_fusion
  11.7 0.0 copy-start.1
  11.8 0.0 all-reduce.9.cloned.1.call-update
  11.8 0.0 all-reduce.5.cloned.1.call-start
  11.8 1.1 copy-done.1
  13.0 0.1 copy.8
  13.1 45.1 %all_to_all.19 = f32[128,8,256]{2,0,1:T(8,128)S(1)} all-to-all(f32[128,8,256]{2,0,1:T(8,128)S(1)} %bitcast.31), channel_id=1, replica_groups=mesh['rows'=64,'cols'=8] {'cols'}, dimensions={1} | all-to-all | bytes 2097152 | tf_op jit(solution)/shard_map/all_to_all | solution.py:17
  58.2 58.0 %all-reduce.9.cloned.1.call-done = (f32[1024,256]{1,0:T(8,128)}, f32[1024,256]{1,0:T(8,128)}) async-done(((f32[1024,256]{1,0:T(8,128)}, f32[1024,256]{1,0:T(8,128)}), (f32[1024,256]{1,0:T(8,128)}, f32[1024,256]{1,0:T(8,128)})) %all-reduce.9.cloned.1.call-update) | async-done | bytes 2097168 | tf_op jit(solution)/shard_map/psum | solution.py:9
  116.2 0.0 copy-start.2
  116.2 3.8 fusion.11
  120.0 0.0 all-reduce.5.cloned.1.call-update
  120.0 0.0 all-reduce.7.cloned.1.call-start
  120.0 188.2 %all-reduce.5.cloned.1.call-done = f32[256,256]{1,0:T(8,128)} async-done(((f32[256,256]{1,0:T(8,128)}), f32[256,256]{1,0:T(8,128)}) %all-reduce.5.cloned.1.call-update) | async-done | bytes 262160 | tf_op jit(solution)/shard_map/psum | solution.py:26
  308.2 0.0 copy-done.2
  308.2 1.4 fusion.1
  309.6 0.0 copy-start
  309.6 2.3 convolution_subtract_fusion.1
  311.9 0.0 copy-done
  311.9 0.0 copy-start.3
  312.0 2.5 fusion.12
  314.5 0.0 all-reduce.7.cloned.1.call-update
  314.5 184.1 %all-reduce.7.cloned.1.call-done = f32[256,256]{1,0:T(8,128)} async-done(((f32[256,256]{1,0:T(8,128)}), f32[256,256]{1,0:T(8,128)}) %all-reduce.7.cloned.1.call-update) | async-done | bytes 262160 | tf_op jit(solution)/shard_map/psum | solution.py:26
  498.6 0.0 copy-done.3
  498.6 1.4 fusion
  500.0 2.0 convolution_subtract_fusion
  (1 shorter events, 0.0 us)
Async XLA Ops:
  6.5 109.6 %all-reduce.9.cloned.1.call-start = ((), (), s32[]{:S(2)}) async-start(), calls=%async_computation.3 | async-start | bytes 4194304 | tf_op jit(solution)/shard_map/psum | solution.py:9
  6.5 0.7 copy-start.4
  11.7 1.2 copy-start.1
  11.8 296.5 %all-reduce.5.cloned.1.call-start = ((), (), s32[]{:S(2)}) async-start(), calls=%async_computation.1 | async-start | bytes 524288 | tf_op jit(solution)/shard_map/psum | solution.py:26
  116.2 192.1 %copy-start.2 = (f32[2,256,256]{2,1,0:T(8,128)S(1)}, f32[2,256,256]{2,1,0:T(8,128)}, u32[]{:S(2)}) copy-start(f32[2,256,256]{2,1,0:T(8,128)} %param.6) | copy-start | bytes 1572868
  120.0 378.7 %all-reduce.7.cloned.1.call-start = ((), (), s32[]{:S(2)}) async-start(), calls=%async_computation.2 | async-start | bytes 524288 | tf_op jit(solution)/shard_map/psum | solution.py:26
  309.6 2.3 copy-start
  311.9 186.7 %copy-start.3 = (f32[2,256,256]{2,1,0:T(8,128)S(1)}, f32[2,256,256]{2,1,0:T(8,128)}, u32[]{:S(2)}) copy-start(f32[2,256,256]{2,1,0:T(8,128)} %param.6) | copy-start | bytes 1572868
Sparse Core Ops, SparseCore 0:
  11.9 104.2 all-reduce.8
  120.1 188.0 all-reduce.4
  314.6 183.9 all-reduce.6
where the time goes:
time: 509 us
  waiting for transfers between devices  430 us (84%)
  blocking collectives  45.1 us (9%)
  between operations  14.5 us (3%)
  matrix products  13.3 us (3%)
    psum x2, waiting for transfers between devices, per_device(): proj = lax.psum(matmul(vectors[index].T, result), 'rows')  372 us
    psum x1, waiting for transfers between devices, broadcast(): return lax.psum(jnp.where(mine, x, jnp.zeros_like(x)), axis)  58 us
    all_to_all x1, blocking collectives, per_device(): lax.all_to_all(eigvecs, 'cols', split_axis=1, concat_axis=0, tiled=True)  45.1 us
    dot_general x6, matrix products, matmul(): jnp.dot(left, right, precision=lax.Precision.HIGHEST, preferred_element_t...  13.3 us
  transfers between devices with their start and end apart: 3, of which 3 were waited for; matrix products, arithmetic and copies ran while one was open for 0% of the time, Pallas kernels for 0%

commit v1 on v0

--- a/solution.py
+++ b/solution.py
@@ -6,7 +6,7 @@
 
 def broadcast(x, axis, root):
     mine = lax.axis_index(axis) == root
-    return lax.psum(jnp.where(mine, x, jnp.zeros_like(x)), axis)
+    return jnp.sum(lax.all_gather(jnp.where(mine, x, jnp.zeros_like(x)), axis), axis=0)
 
 
 def matmul(left, right):

time: 509 us -> 620 us (1.22)
  waiting for transfers between devices: 430 us -> 567 us
  blocking collectives: 45.1 us -> 0 us
  starting transfers between devices: 0.09 us -> 11 us
  other arithmetic: 2.7 us -> 10.8 us
    all_gather x0 -> x2, waiting for transfers between devices: none -> 197 us  [broadcast(): lax.all_gather(jnp.where(mine, x, jnp.zeros_like(x)), axis)]
    psum x1 -> x0, waiting for transfers between devices: 58 us -> none  [broadcast(): return lax.psum(jnp.where(mine, x, jnp.zeros_like(x)), axis)]
    all_to_all x1 -> x0, blocking collectives: 45.1 us -> none  [per_device(): lax.all_to_all(eigvecs, 'cols', split_axis=1, concat_axis=0, tiled=True)]
    all_to_all x0 -> x1, starting transfers between devices: none -> 10.9 us  [per_device(): lax.all_to_all(eigvecs, 'cols', split_axis=1, concat_axis=0, tiled=True)]
    reduce_sum x0 -> x2, other arithmetic: none -> 8.12 us  [broadcast(): jnp.sum(lax.all_gather(jnp.where(mine, x, jnp.zeros_like(x)), axis), axis=0)]
  transfers between devices with their start and end apart: 3 -> 5, of which waited for: 3 -> 4; matrix products, arithmetic and copies ran while one was open for 0% -> 2% of each run, Pallas kernels for 0% -> 0%
where the time goes in v1:
time: 620 us
  waiting for transfers between devices  567 us (91%)
  between operations  14.4 us (2%)
  matrix products  12.1 us (2%)
  starting transfers between devices  11 us (2%)
  other arithmetic  10.8 us (2%)
    psum x2, waiting for transfers between devices, per_device(): proj = lax.psum(matmul(vectors[index].T, result), 'rows')  368 us
    all_gather x2, waiting for transfers between devices, broadcast(): lax.all_gather(jnp.where(mine, x, jnp.zeros_like(x)), axis)  197 us
  transfers between devices with their start and end apart: 5, of which 4 were waited for; matrix products, arithmetic and copies ran while one was open for 2% of the time, Pallas kernels for 0%

profile of v1, /device:TPU:1, one launch (start us, length us, event | category | flops | bytes accessed | tf_op | source)
XLA Modules:
  0.0 619.5 jit_solution(8926246261734107966)
XLA Ops:
  6.5 0.0 all-gather.3.cloned.1.call-start
  6.5 1.3 fusion.10
  9.1 2.7 broadcast_select_fusion
  11.8 0.0 all-gather.3.cloned.1.call-update
  11.8 0.0 all-gather.5.cloned.1.call-start
  11.8 0.7 all-gather.5.cloned.1.call-update
  12.6 2.3 copy.9
  14.8 10.9 %all-to-all-start = ((f32[128,8,256]{2,0,1:T(8,128)}), f32[128,8,256]{2,0,1:T(8,128)S(1)}, u32[]{:S(2)}, u32[]{:S(2)}) async-start(f32[128,8,256]{2,0,1:T(8,128)} %bitcast.24), calls=%async_computation | async-start | bytes 2097152 | tf_op jit(solution)/shard_map/all_to_all | solution.py:17
  25.7 0.0 all-reduce.3.cloned.1.call-start
  25.8 105.8 %all-gather.3.cloned.1.call-done = f32[8,1024,256]{2,1,0:T(8,128)} async-done(((f32[1,1024,256]{2,1,0:T(8,128)}), f32[8,1024,256]{2,1,0:T(8,128)}) %all-gather.3.cloned.1.call-update) | async-done | bytes 8388624 | tf_op jit(solution)/shard_map/all_gather | solution.py:9
  131.5 4.1 reduce_sum.18
  135.6 0.0 all-to-all-done
  135.6 2.5 fusion.11
  138.1 0.0 all-reduce.3.cloned.1.call-update
  138.2 0.0 all-reduce.5.cloned.1.call-start
  138.2 91.7 %all-gather.5.cloned.1.call-done = f32[8,1024,256]{2,1,0:T(8,128)} async-done(((f32[1,1024,256]{2,1,0:T(8,128)}), f32[8,1024,256]{2,1,0:T(8,128)}) %all-gather.5.cloned.1.call-update) | async-done | bytes 8388624 | tf_op jit(solution)/shard_map/all_gather | solution.py:9
  229.9 4.1 reduce_sum.19
  233.9 184.2 %all-reduce.3.cloned.1.call-done = f32[256,256]{1,0:T(8,128)} async-done(((f32[256,256]{1,0:T(8,128)}), f32[256,256]{1,0:T(8,128)}) %all-reduce.3.cloned.1.call-update) | async-done | bytes 262160 | tf_op jit(solution)/shard_map/psum | solution.py:26
  418.1 1.4 fusion.1
  419.5 1.0 convolution_subtract_fusion.1
  420.5 0.0 copy-start
  420.6 1.0 copy-done
  421.5 2.5 fusion.12
  424.0 0.0 all-reduce.5.cloned.1.call-update
  424.1 184.3 %all-reduce.5.cloned.1.call-done = f32[256,256]{1,0:T(8,128)} async-done(((f32[256,256]{1,0:T(8,128)}), f32[256,256]{1,0:T(8,128)}) %all-reduce.5.cloned.1.call-update) | async-done | bytes 262160 | tf_op jit(solution)/shard_map/psum | solution.py:26
  608.3 1.4 fusion
  609.8 3.2 convolution_subtract_fusion
  (1 shorter events, 0.0 us)
Async XLA Ops:
  6.5 125.0 %all-gather.3.cloned.1.call-start = ((), (), s32[]{:S(2)}) async-start(), calls=%async_computation.1 | async-start | bytes 9437184 | tf_op jit(solution)/shard_map/all_gather | solution.py:9
  11.8 218.1 %all-gather.5.cloned.1.call-start = ((), (), s32[]{:S(2)}) async-start(), calls=%async_computation.3 | async-start | bytes 9437184 | tf_op jit(solution)/shard_map/all_gather | solution.py:9
  14.8 120.7 %all-to-all-start = ((f32[128,8,256]{2,0,1:T(8,128)}), f32[128,8,256]{2,0,1:T(8,128)S(1)}, u32[]{:S(2)}, u32[]{:S(2)}) async-start(f32[128,8,256]{2,0,1:T(8,128)} %bitcast.24), calls=%async_computation | async-start | bytes 2097152 | tf_op jit(solution)/shard_map/all_to_all | solution.py:17
  25.7 392.4 %all-reduce.3.cloned.1.call-start = ((), (), s32[]{:S(2)}) async-start(), calls=%async_computation.2 | async-start | bytes 524288 | tf_op jit(solution)/shard_map/psum | solution.py:26
  138.2 470.2 %all-reduce.5.cloned.1.call-start = ((), (), s32[]{:S(2)}) async-start(), calls=%async_computation.4 | async-start | bytes 524288 | tf_op jit(solution)/shard_map/psum | solution.py:26
  420.5 1.0 copy-start
Sparse Core Ops, SparseCore 0:
  11.9 119.5 all-gather.2
  133.6 96.2 all-gather.4
  233.4 184.6 all-reduce.2
  424.2 184.1 all-reduce.4
